TPU v7x, 256 devices: a whole 4x4x8 slice. The times are simulated.
256 devices in a mesh: ctx: 64 (over z, x, core), rows: 4 (over y).
Axes of the slice: x: 4, y: 4, z: 8, core: 2. Of those that a mesh axis runs over, the one named last changes fastest.
Arguments:
- hidden: bfloat16 [2, 4, 8192], P(None, 'rows'), may hold values from -6 to 6
- norm_gain: bfloat16 [8192], replicated, may hold values from 0.099609375 to 1.8984375
- w_query: bfloat16 [8192, 8192], P(None, 'ctx'), may hold values from -2 to 2
- w_key: bfloat16 [8192, 1024], P(None, 'ctx'), may hold values from -2 to 2
- w_value: bfloat16 [8192, 1024], P(None, 'ctx'), may hold values from -0.0625 to 0.0625
- w_out: bfloat16 [8192, 8192], P('ctx'), may hold values from -0.0625 to 0.0625
- cache_keys: bfloat16 [4, 131072, 8, 128], P('rows', 'ctx'), may hold values from -1200 to 1200
- cache_values: bfloat16 [4, 131072, 8, 128], P('rows', 'ctx'), may hold values from -24 to 24
- lengths: int32 [4], P('rows'), may hold values from 1 to 131072, as said below
- positions: int32 [4], P('rows'), may hold values from 0 to 8191
Outputs:
- attended: bfloat16 [2, 8192, 4], P(None, 'ctx', 'rows')
Inputs may be any that keep to these rules, and one draw needn't show every extreme that they name: `lengths`: one sequence has exactly 131072 live tokens and another at most 32; slots at or past a sequence's length hold entries that must not be read.
All inputs are finite; a program needn't handle non-finite values.
Results may differ from a plain program's by a relative error of at most 0.02.
The roundings to bfloat16 on the way count: a program that leaves them out, or rounds other values in their place, can miss the bound.
Values may be sent and summed in bfloat16 or wider, within the bound.
A program may use at most 64 MiB of HBM per device.

v0:
```python
import math

import jax
import jax.numpy as jnp
from jax import lax
from jax.sharding import PartitionSpec as P

theta_base = 500000.0
epsilon = 1e-05


def in_one_piece(arrays, axis, dim, along):
    widths = [a.shape[along] for a in arrays]
    both = jnp.concatenate(arrays, axis=along)
    whole = lax.all_gather(both, axis, axis=dim, tiled=True)
    return tuple(jnp.split(whole, [sum(widths[:k]) for k in range(1, len(widths))], axis=along))


def in_one_piece_2(arrays, axis, split_dim, concat_dim, along):
    widths = [math.prod(a.shape[along:]) for a in arrays]
    both = jnp.concatenate(
        [a.reshape(*a.shape[:along], w) for a, w in zip(arrays, widths)], axis=along
    )
    whole = lax.all_to_all(both, axis, split_axis=split_dim, concat_axis=concat_dim, tiled=True)
    tiles = jnp.split(whole, [sum(widths[:k]) for k in range(1, len(widths))], axis=along)
    return tuple((b.reshape(*whole.shape[:along], *a.shape[along:]) for a, b in zip(arrays, tiles)))


def in_blocks(shard, dim, peers):
    shape = shard.shape
    tiles = shard.reshape(*shape[:dim], peers, shape[dim] // peers, *shape[dim + 1 :])
    return jnp.moveaxis(tiles, dim, 0)


def sum_at_owner(shard, axis, dim):
    tiles = in_blocks(shard, dim, lax.axis_size(axis))
    arrived = lax.all_to_all(tiles, axis, split_axis=0, concat_axis=0, tiled=True)
    return arrived.sum(axis=0)


def rotate(vectors, places):
    halfway = vectors.shape[-1] // 2
    inverse = theta_base ** (-(jnp.arange(halfway, dtype=jnp.float32) * 2.0 / vectors.shape[-1]))
    angles = places.astype(jnp.float32)[:, None, None] * inverse
    cosines = jnp.cos(angles)
    sines = jnp.sin(angles)
    leading = vectors[..., :halfway]
    trailing = vectors[..., halfway:]
    return jnp.concatenate(
        [leading * cosines - trailing * sines, trailing * cosines + leading * sines], -1
    )


def normalize(inputs, norm_gain):
    scaled = inputs * lax.rsqrt(jnp.mean(inputs * inputs, -1, keepdims=True) + epsilon)
    return (scaled * norm_gain.astype(jnp.float32)).astype(jnp.bfloat16)


def local_part(grouped, cache_keys, cache_values, live_len, block_size, limit, scale_factor):
    row_count, kv_heads, group_size, head_size = grouped.shape

    def one_block(block_index, carried):
        run_max, numer, denom = carried
        key_block = lax.dynamic_slice_in_dim(cache_keys, block_index * block_size, block_size, 1)
        value_block = lax.dynamic_slice_in_dim(
            cache_values, block_index * block_size, block_size, 1
        )
        scores = (
            jnp.einsum("rkgd,rtkd->rkgt", grouped, key_block, preferred_element_type=jnp.float32)
            * scale_factor
        )
        slots = block_index * block_size + jnp.arange(block_size)
        visible = slots[None, None, None, :] < live_len[:, None, None, None]
        scores = jnp.where(visible, scores, -1e30)
        new_max = jnp.maximum(run_max, jnp.max(scores, -1))
        shrink = jnp.exp(run_max - new_max)
        weights = jnp.where(visible, jnp.exp(scores - new_max[..., None]), 0.0)
        denom = denom * shrink + jnp.sum(weights, -1)
        numer = numer * shrink[..., None] + jnp.einsum(
            "rkgt,rtkd->rkgd",
            weights.astype(jnp.bfloat16),
            value_block,
            preferred_element_type=jnp.float32,
        )
        return (new_max, numer, denom)

    initial = (
        jnp.full((row_count, kv_heads, group_size), -1e30, jnp.float32),
        jnp.zeros((row_count, kv_heads, group_size, head_size), jnp.float32),
        jnp.zeros((row_count, kv_heads, group_size), jnp.float32),
    )
    run_max, numer, denom = lax.fori_loop(0, limit, one_block, initial)
    total_heads = kv_heads * group_size
    return (
        run_max.reshape(row_count, total_heads),
        numer.reshape(row_count, total_heads, head_size),
        denom.reshape(row_count, total_heads),
    )


def on_device(
    hidden, norm_gain, w_query, w_key, w_value, w_out, cache_keys, cache_values, lengths, positions
):
    devices = lax.axis_size("ctx")
    ctx_index = lax.axis_index("ctx")
    step_count = hidden.shape[0]
    row_count = hidden.shape[1]
    head_size = cache_keys.shape[3]
    kv_heads = cache_keys.shape[2]
    local_span = cache_keys.shape[1]
    own_heads = w_query.shape[1] // head_size
    total_heads = own_heads * devices
    group_size = total_heads // kv_heads
    scale_factor = 1.0 / math.sqrt(head_size)
    block_size = min(512, local_span)
    limit = local_span // block_size
    live_len = jnp.clip(lengths - ctx_index * local_span, 0, local_span)
    head_start = ctx_index * own_heads
    kv_index = head_start // group_size
    fresh_keys = []
    fresh_values = []
    results = []
    for step_index in range(step_count):
        layer_in = hidden[step_index].astype(jnp.float32)
        normed = normalize(layer_in, norm_gain)
        query_local = jnp.dot(normed, w_query, preferred_element_type=jnp.float32).astype(
            jnp.bfloat16
        )
        key_local = jnp.dot(normed, w_key, preferred_element_type=jnp.float32).astype(jnp.bfloat16)
        value_local = jnp.dot(normed, w_value, preferred_element_type=jnp.float32).astype(
            jnp.bfloat16
        )
        query_all, key_all, value_all = (
            lax.all_gather(query_local, "ctx", axis=1, tiled=True),
            *in_one_piece((key_local, value_local), "ctx", 1, 0),
        )
        places = positions + step_index
        queries = rotate(
            query_all.astype(jnp.float32).reshape(row_count, total_heads, head_size), places
        ).astype(jnp.bfloat16)
        new_keys = rotate(
            key_all.astype(jnp.float32).reshape(row_count, kv_heads, head_size), places
        ).astype(jnp.bfloat16)
        fresh_keys.append(new_keys)
        fresh_values.append(value_all.reshape(row_count, kv_heads, head_size))
        grouped = queries.reshape(row_count, kv_heads, group_size, head_size)
        run_max, numer, denom = local_part(
            grouped, cache_keys, cache_values, live_len, block_size, limit, scale_factor
        )
        got_max, got_num, got_den = tuple(
            (
                part.astype(jnp.float32)
                for part in in_one_piece_2(
                    (
                        run_max.astype(jnp.bfloat16),
                        numer.astype(jnp.bfloat16),
                        denom.astype(jnp.bfloat16),
                    ),
                    "ctx",
                    1,
                    1,
                    2,
                )
            )
        )
        got_max = got_max.reshape(row_count, devices, own_heads)
        got_num = got_num.reshape(row_count, devices, own_heads, head_size)
        got_den = got_den.reshape(row_count, devices, own_heads)
        own_max = jnp.max(got_max, 1)
        factors = jnp.exp(got_max - own_max[:, None, :])
        own_num = jnp.sum(got_num * factors[..., None], 1)
        own_den = jnp.sum(got_den * factors, 1)
        own_query = lax.dynamic_slice_in_dim(queries, head_start, own_heads, 1)
        stacked_keys = lax.dynamic_index_in_dim(
            jnp.stack(fresh_keys, 1), kv_index, 2, keepdims=False
        )
        stacked_values = lax.dynamic_index_in_dim(
            jnp.stack(fresh_values, 1), kv_index, 2, keepdims=False
        )
        fresh_scores = (
            jnp.einsum("rjd,rtd->rjt", own_query, stacked_keys, preferred_element_type=jnp.float32)
            * scale_factor
        )
        final_max = jnp.maximum(own_max, jnp.max(fresh_scores, -1))
        shrink = jnp.exp(own_max - final_max)
        fresh_weights = jnp.exp(fresh_scores - final_max[..., None])
        final_den = own_den * shrink + jnp.sum(fresh_weights, -1)
        final_num = own_num * shrink[..., None] + jnp.einsum(
            "rjt,rtd->rjd",
            fresh_weights.astype(jnp.bfloat16),
            stacked_values,
            preferred_element_type=jnp.float32,
        )
        head_out = (
            (final_num / final_den[..., None])
            .astype(jnp.bfloat16)
            .reshape(row_count, own_heads * head_size)
        )
        summed = sum_at_owner(
            lax.dot_general(
                w_out, head_out, (((0,), (1,)), ((), ())), preferred_element_type=jnp.float32
            ),
            "ctx",
            0,
        )
        results.append(summed.astype(jnp.bfloat16))
    return jnp.stack(results, 0)


def solution(mesh):
    in_specs = (
        P(None, "rows", None),
        P(),
        P(None, "ctx"),
        P(None, "ctx"),
        P(None, "ctx"),
        P("ctx", None),
        P("rows", "ctx", None, None),
        P("rows", "ctx", None, None),
        P("rows"),
        P("rows"),
    )
    out_specs = P(None, "ctx", "rows")
    return jax.shard_map(
        on_device, mesh=mesh, in_specs=in_specs, out_specs=out_specs, check_vma=False
    )
```

profile of v0, /device:TPU:1, one launch (start us, length us, event | category | flops | bytes accessed | tf_op | source)
XLA Modules:
  0.0 265.3 jit_solution(8186538398806153378)
XLA Ops:
  0.0 1.7 multiply_reduce_fusion.1
  3.1 0.9 convert_multiply_fusion.3
  4.0 0.7 fusion.65
  5.5 2.0 fusion.59
  7.5 44.0 %all-gather.2 = bf16[64,1,128]{2,1,0:T(2,128)(2,1)S(1)} all-gather(bf16[1,1,128]{2,1,0:T(2,128)(2,1)S(1)} %fusion.59), channel_id=2, replica_groups=mesh['ctx'=64,'rows'=4] {'ctx'}, dimensions={0}, use_global_device_ids=true | all-gather | bytes 16640 | tf_op jit(solution)/shard_map/all_gather | solution.py:134
  52.1 4.8 %copy.55 = bf16[1,2048,8,128]{3,1,2,0:T(8,128)(2,1)} copy(bf16[1,2048,8,128]{3,2,1,0:T(8,128)(2,1)} %param.20) | data formatting | bytes 8388608
  57.0 2.6 copy.56
  59.8 14.0 %while.36 = (s32[]{:T(128)}, f32[1,8,8]{2,1,0:T(8,128)S(1)}, f32[1,8,8,128]{3,2,1,0:T(8,128)S(1)}, f32[1,8,8]{2,1,0:T(8,128)S(1)}, s32[1]{0:T(128)}, /*index=5*/...) while((s32[]{:T(128)}, f32[1,8,8]{2,1,0:T(8,128)S(1)}, ...), condition=%wide.region_4.5_spmd.clone, body=%wide.region_1.4_spmd.clone.sunk | while | flops 17098120 | bytes 2578623 | solution.py:92
  59.8 1.7 fusion.143
  61.6 1.6 fusion.145
  63.1 0.2 fusion.146
  63.3 1.7 fusion.143
  65.0 1.6 fusion.145
  66.6 0.2 fusion.146
  66.8 1.7 fusion.143
  68.5 1.6 fusion.145
  70.1 0.2 fusion.146
  70.3 1.7 fusion.143
  72.0 1.6 fusion.145
  73.6 0.2 fusion.146
  74.1 0.7 copy.59
  74.8 6.4 %all-to-all-start = ((bf16[1,64,130]{2,0,1:T(2,128)(2,1)}), bf16[1,64,130]{2,0,1:T(2,128)(2,1)S(1)}, u32[]{:S(2)}, u32[]{:S(2)}) async-start(bf16[1,64,130]{2,0,1:T(2,128)(2,1)} %copy.59), calls=%async_computation | async-start | bytes 131072 | tf_op jit(solution)/shard_map/all_to_all | solution.py:24
  81.2 0.2 fusion.55
  81.4 0.2 fusion.57
  81.7 0.2 fusion.49
  81.9 0.2 fusion.51
  82.1 2.0 fusion.53
  84.1 41.3 %all-gather.3 = bf16[64,16,2]{1,2,0:T(2,128)(2,1)S(1)} all-gather(bf16[1,16,2]{1,2,0:T(2,128)(2,1)S(1)} %maximum_bitcast_fusion), channel_id=1, replica_groups=mesh['ctx'=64,'rows'=4] {'ctx'}, dimensions={0}, use_global_device_ids=true | all-gather | bytes 4160 | tf_op jit(solution)/shard_map/all_gather | solution.py:15
  125.4 0.1 reshape.834
  125.5 37.3 %all-gather.5 = bf16[64,16,2]{1,2,0:T(2,128)(2,1)S(1)} all-gather(bf16[1,16,2]{1,2,0:T(2,128)(2,1)S(1)} %maximum_bitcast_fusion.1), channel_id=1, replica_groups=mesh['ctx'=64,'rows'=4] {'ctx'}, dimensions={0}, use_global_device_ids=true | all-gather | bytes 4160 | tf_op jit(solution)/shard_map/all_gather | solution.py:15
  162.9 0.1 reshape.838
  163.2 38.0 %all-gather.4 = bf16[64,1,128]{2,1,0:T(2,128)(2,1)S(1)} all-gather(bf16[1,1,128]{2,1,0:T(2,128)(2,1)S(1)} %fusion.53), channel_id=3, replica_groups=mesh['ctx'=64,'rows'=4] {'ctx'}, dimensions={0}, use_global_device_ids=true | all-gather | bytes 16640 | tf_op jit(solution)/shard_map/all_gather | solution.py:134
  201.5 13.9 %while.37 = (s32[]{:T(128)}, f32[1,8,8]{2,1,0:T(8,128)S(1)}, f32[1,8,8,128]{3,2,1,0:T(8,128)S(1)}, f32[1,8,8]{2,1,0:T(8,128)S(1)}, s32[1]{0:T(128)}, /*index=5*/...) while((s32[]{:T(128)}, f32[1,8,8]{2,1,0:T(8,128)S(1)}, ...), condition=%wide.region_13.14_spmd.clone, body=%wide.region_10.13_spmd.clone.sunk | while | flops 17098120 | bytes 2578623 | solution.py:92
  201.5 1.7 fusion.149
  203.2 1.6 fusion.151
  204.7 0.2 fusion.152
  205.0 1.7 fusion.149
  206.7 1.6 fusion.151
  208.2 0.2 fusion.152
  208.5 1.7 fusion.149
  210.2 1.6 fusion.151
  211.7 0.2 fusion.152
  212.0 1.7 fusion.149
  213.7 1.6 fusion.151
  215.2 0.2 fusion.152
  215.7 0.8 fusion.114
  216.7 0.7 copy.65
  217.3 0.7 fusion.83
  218.7 5.7 %all-to-all-start.2 = ((bf16[1,64,130]{2,0,1:T(2,128)(2,1)}), bf16[1,64,130]{2,0,1:T(2,128)(2,1)S(1)}, u32[]{:S(2)}, u32[]{:S(2)}) async-start(bf16[1,64,130]{2,0,1:T(2,128)(2,1)} %copy.65), calls=%async_computation.2 | async-start | bytes 131072 | tf_op jit(solution)/shard_map/all_to_all | solution.py:24
  224.3 0.7 slice_reduce_fusion.1
  225.7 1.0 fusion.72
  227.4 0.2 fusion.71
  227.7 1.0 fusion.42
  228.7 5.8 %all-to-all-done.2 = bf16[1,64,130]{2,0,1:T(2,128)(2,1)S(1)} async-done(((bf16[1,64,130]{2,0,1:T(2,128)(2,1)}), bf16[1,64,130]{2,0,1:T(2,128)(2,1)S(1)}, u32[]{:S(2)}, u32[]{:S(2)}) %all-to-all-start.2) | async-done | bytes 16672 | tf_op jit(solution)/shard_map/all_to_all | solution.py:24
  234.4 4.5 %all-to-all-start.1 = ((f32[64,128,1]{1,2,0:T(1,128)}), f32[64,128,1]{1,2,0:T(1,128)S(1)}, u32[]{:S(2)}, u32[]{:S(2)}) async-start(f32[64,128,1]{1,2,0:T(1,128)} %fusion.42), calls=%async_computation.1 | async-start | bytes 65536 | tf_op jit(solution)/shard_map/all_to_all | solution.py:37
  239.0 0.7 slice_reduce_fusion
  240.9 0.6 fusion.109
  241.5 1.0 fusion.74
  243.7 0.2 fusion.73
  243.9 1.1 fusion.45
  245.0 3.3 %all-to-all-done.1 = f32[64,128,1]{1,2,0:T(1,128)S(1)} async-done(((f32[64,128,1]{1,2,0:T(1,128)}), f32[64,128,1]{1,2,0:T(1,128)S(1)}, u32[]{:S(2)}, u32[]{:S(2)}) %all-to-all-start.1) | async-done | bytes 32800 | tf_op jit(solution)/shard_map/all_to_all | solution.py:37
  248.3 7.0 %all-to-all-start.3 = ((f32[64,128,1]{1,2,0:T(1,128)}), f32[64,128,1]{1,2,0:T(1,128)S(1)}, u32[]{:S(2)}, u32[]{:S(2)}) async-start(f32[64,128,1]{1,2,0:T(1,128)} %fusion.45), calls=%async_computation.3 | async-start | bytes 65536 | tf_op jit(solution)/shard_map/all_to_all | solution.py:37
  255.4 9.3 %all-to-all-done.3 = f32[64,128,1]{1,2,0:T(1,128)S(1)} async-done(((f32[64,128,1]{1,2,0:T(1,128)}), f32[64,128,1]{1,2,0:T(1,128)S(1)}, u32[]{:S(2)}, u32[]{:S(2)}) %all-to-all-start.3) | async-done | bytes 32800 | tf_op jit(solution)/shard_map/all_to_all | solution.py:37
  264.8 0.5 copy.69
  (81 shorter events, 1.9 us)
Async XLA Ops:
  0.0 227.7 %copy-start = (bf16[128,8192]{1,0:T(8,128)(2,1)S(1)}, bf16[128,8192]{1,0:T(8,128)(2,1)}, u32[]{:S(2)}) copy-start(bf16[128,8192]{1,0:T(8,128)(2,1)} %param.19) | copy-start | bytes 6291460
  52.1 4.8 %copy-start.1 = (bf16[1,2048,8,128]{3,2,1,0:T(8,128)(2,1)S(1)}, bf16[1,2048,8,128]{3,2,1,0:T(8,128)(2,1)}, u32[]{:S(2)}) copy-start(bf16[1,2048,8,128]{3,2,1,0:T(8,128)(2,1)} %param.21) | copy-start | bytes 12582916
  59.8 21.5 %copy-start.2 = (bf16[8192,16]{0,1:T(8,128)(2,1)S(1)}, bf16[8192,16]{0,1:T(8,128)(2,1)}, u32[]{:S(2)}) copy-start(bf16[8192,16]{0,1:T(8,128)(2,1)} %param.18) | copy-start | bytes 786436
  59.8 21.7 %copy-start.3 = (bf16[8192,16]{0,1:T(8,128)(2,1)S(1)}, bf16[8192,16]{0,1:T(8,128)(2,1)}, u32[]{:S(2)}) copy-start(bf16[8192,16]{0,1:T(8,128)(2,1)} %param.17) | copy-start | bytes 786436
  74.8 143.9 %all-to-all-start = ((bf16[1,64,130]{2,0,1:T(2,128)(2,1)}), bf16[1,64,130]{2,0,1:T(2,128)(2,1)S(1)}, u32[]{:S(2)}, u32[]{:S(2)}) async-start(bf16[1,64,130]{2,0,1:T(2,128)(2,1)} %copy.59), calls=%async_computation | async-start | bytes 131072 | tf_op jit(solution)/shard_map/all_to_all | solution.py:24
  218.7 15.7 %all-to-all-start.2 = ((bf16[1,64,130]{2,0,1:T(2,128)(2,1)}), bf16[1,64,130]{2,0,1:T(2,128)(2,1)S(1)}, u32[]{:S(2)}, u32[]{:S(2)}) async-start(bf16[1,64,130]{2,0,1:T(2,128)(2,1)} %copy.65), calls=%async_computation.2 | async-start | bytes 131072 | tf_op jit(solution)/shard_map/all_to_all | solution.py:24
  234.4 13.9 %all-to-all-start.1 = ((f32[64,128,1]{1,2,0:T(1,128)}), f32[64,128,1]{1,2,0:T(1,128)S(1)}, u32[]{:S(2)}, u32[]{:S(2)}) async-start(f32[64,128,1]{1,2,0:T(1,128)} %fusion.42), calls=%async_computation.1 | async-start | bytes 65536 | tf_op jit(solution)/shard_map/all_to_all | solution.py:37
  248.3 16.4 %all-to-all-start.3 = ((f32[64,128,1]{1,2,0:T(1,128)}), f32[64,128,1]{1,2,0:T(1,128)S(1)}, u32[]{:S(2)}, u32[]{:S(2)}) async-start(f32[64,128,1]{1,2,0:T(1,128)} %fusion.45), calls=%async_computation.3 | async-start | bytes 65536 | tf_op jit(solution)/shard_map/all_to_all | solution.py:37
where the time goes:
time: 267 us; the launch traced here: 265 us
  blocking collectives  161 us (60%)
  matrix products  33.6 us (13%)
  starting transfers between devices  23.6 us (9%)
  waiting for transfers between devices  18.3 us (7%)
  other arithmetic  11.3 us (4%)
  local copies, waits for them, and re-layouts  9.95 us (4%)
  between operations  7.52 us (3%)
    all_gather x2, blocking collectives, on_device(): lax.all_gather(query_local, 'ctx', axis=1, tiled=True)  82 us
    all_gather x2, blocking collectives, in_one_piece(): whole = lax.all_gather(both, axis, axis=dim, tiled=True)  78.6 us
    dot_general x8, matrix products, one_block(): jnp.einsum('rkgd,rtkd->rkgt', grouped, key_block, preferred_element_type=...  13.5 us
    all_to_all x2, waiting for transfers between devices, sum_at_owner(): lax.all_to_all(tiles, axis, split_axis=0, concat_axis=0, tiled=True)  12.6 us
    dot_general x8, matrix products, one_block(): jnp.einsum('rkgt,rtkd->rkgd', weights.astype(jnp.bfloat16), value_block,...  12.4 us
    all_to_all x2, starting transfers between devices, in_one_piece_2(): lax.all_to_all(both, axis, split_axis=split_dim, concat_axis=concat_dim,...  12.1 us
    all_to_all x2, starting transfers between devices, sum_at_owner(): lax.all_to_all(tiles, axis, split_axis=0, concat_axis=0, tiled=True)  11.5 us
    unnamed x12, local copies, waits for them, and re-layouts  7.67 us
  transfers between devices with their start and end apart: 4, of which 3 were waited for; matrix products, arithmetic and copies ran while one was open for 10% of the time, Pallas kernels for 0%

commit v1 on v0

v1 whole, which is shorter than its diff:
```python
import functools
import math

import jax
import jax.numpy as jnp
import numpy as np
from jax import lax
from jax.experimental import pallas as pl
from jax.experimental.pallas import tpu as pltpu
from jax.sharding import PartitionSpec as P

theta_base = 500000.0
epsilon = 1e-05
NEG = -1e30
LANES = 128
MESH = pl.DeviceIdType.MESH
F32 = jnp.float32
BF16 = jnp.bfloat16


def to(peer):
    return {"ctx": peer}


def lane_class_reduce(x, op, period):
    shift = period
    while shift < LANES:
        x = op(x, pltpu.roll(x, shift, 1))
        shift *= 2
    return x


def kernel(
    dims,
    pos_hbm, len_hbm, hid_hbm, gain_hbm, inv_hbm, wq_hbm, wk_hbm, wv_hbm, wo_hbm, kc_hbm, vc_hbm,
    out_ref,
    pos_s, len_s, hid, gain, inv, wq, wk, wv, wo, kc, vc,
    q_in, kv_out, kv_in, scores, part_out, part_in, proj_out, proj_in,
    load_sem, send_sem, recv_sem,
):
    n, group, steps, chunks, scale = dims
    me = lax.axis_index("ctx")
    plane = me // group
    seat = me % group
    rows = 2 * group
    total = kc.shape[0]
    width = total // chunks

    loads = {}
    pairs = (
        (hid_hbm, hid), (gain_hbm, gain), (pos_hbm, pos_s), (len_hbm, len_s), (inv_hbm, inv),
        (wq_hbm, wq), (wk_hbm, wk), (wv_hbm, wv), (kc_hbm, kc), (vc_hbm, vc), (wo_hbm, wo),
    )
    names = ("hid", "gain", "pos", "len", "inv", "wq", "wk", "wv", "kc", "vc", "wo")
    for i, (name, (src, dst)) in enumerate(zip(names, pairs)):
        loads[name] = pltpu.make_async_copy(src, dst, load_sem.at[i])
        loads[name].start()

    barrier = pltpu.get_barrier_semaphore()

    def greet(p, carry):
        pl.semaphore_signal(barrier, inc=1, device_id=to((me + p) % n), device_id_type=MESH)
        return carry

    lax.fori_loop(1, n, greet, 0)

    loads["hid"].wait()
    loads["gain"].wait()
    x = hid[...].astype(F32)
    x = x * lax.rsqrt(jnp.mean(x * x, -1, keepdims=True) + epsilon)
    normed = jnp.concatenate(
        [
            (x[:, LANES * r : LANES * (r + 1)] * gain[r : r + 1, :].astype(F32)).astype(BF16)
            for r in range(gain.shape[0])
        ],
        axis=1,
    )
    loads["pos"].wait()
    loads["inv"].wait()
    step_row = lax.broadcasted_iota(jnp.int32, (steps, LANES), 0)
    lane2 = lax.broadcasted_iota(jnp.int32, (steps, LANES), 1)
    angles = (pos_s[0] + step_row).astype(F32) * inv[0:1, :]
    cosines = jnp.cos(angles)
    sines = jnp.where(lane2 < LANES // 2, -1.0, 1.0) * jnp.sin(angles)

    def rotary(u):
        return (u * cosines + pltpu.roll(u, LANES // 2, 1) * sines).astype(BF16)

    nt = (((1,), (1,)), ((), ()))
    loads["wk"].wait()
    loads["wv"].wait()
    kv_out[...] = jnp.zeros(kv_out.shape, BF16)
    wide = wk.shape[0]
    kv_out[0:2, 0:wide] = lax.dot_general(normed, wk[...], nt, preferred_element_type=F32).astype(BF16)
    kv_out[2:4, 0:wide] = lax.dot_general(normed, wv[...], nt, preferred_element_type=F32).astype(BF16)
    loads["wq"].wait()
    raw = jnp.dot(normed, wq[...], preferred_element_type=F32).astype(BF16).astype(F32)
    q_own = rotary(raw)
    q_in[me] = q_own
    kv_in[seat] = kv_out[...]

    pl.semaphore_wait(barrier, n - 1)

    def send_q(p, carry):
        pltpu.make_async_remote_copy(
            q_in.at[me], q_in.at[me], send_sem.at[0], recv_sem.at[0],
            device_id=to((me + p) % n), device_id_type=MESH,
        ).start()
        return carry

    lax.fori_loop(1, n, send_q, 0)

    def send_kv(p, carry):
        pltpu.make_async_remote_copy(
            kv_out, kv_in.at[seat], send_sem.at[1], recv_sem.at[1],
            device_id=to(plane * group + (seat + p) % group), device_id_type=MESH,
        ).start()
        return carry

    lax.fori_loop(1, group, send_kv, 0)

    def wait_all(buf, count, k):
        views = buf.at[pl.ds(0, count)]
        both = pltpu.make_async_remote_copy(
            views, views, send_sem.at[k], recv_sem.at[k],
            device_id=to((me + 1) % n), device_id_type=MESH,
        )
        both.wait_recv()
        both.wait_send()

    loads["kc"].wait()
    loads["len"].wait()
    wait_all(q_in, n - 1, 0)

    live = jnp.clip(len_s[0] - me * (total // group), 0, total // group) * group
    lane_w = lax.broadcasted_iota(jnp.int32, (rows, width), 1)
    head_w = lane_w % group
    queries = q_in[...].reshape(n * steps, LANES)

    def score(c, top):
        keys = kc[pl.ds(pl.multiple_of(c * width, width), width), :]
        every = lax.dot_general(queries, keys, nt, preferred_element_type=F32)
        mine = every[0:rows]
        for g in range(1, n // group):
            mine = jnp.where(head_w == g, every[rows * g : rows * (g + 1)], mine)
        mine = jnp.where(lane_w + c * width < live, mine * scale, NEG)
        scores[c] = mine
        for t in range(width // LANES):
            top = jnp.maximum(top, mine[:, LANES * t : LANES * (t + 1)])
        return top

    top = lax.fori_loop(0, chunks, score, jnp.full((rows, LANES), NEG, F32))
    top = lane_class_reduce(top, jnp.maximum, group)

    loads["vc"].wait()
    lane_r = lax.broadcasted_iota(jnp.int32, (rows, LANES), 1)
    picks = [jnp.where(lane_r % group == g, 1.0, 0.0).astype(BF16) for g in range(n // group)]

    def weigh(c, carried):
        den, num = carried
        tiles = []
        for t in range(width // LANES):
            s = scores[c, :, LANES * t : LANES * (t + 1)]
            w = jnp.where(lane_r + (c * width + LANES * t) < live, jnp.exp(s - top), 0.0)
            den = den + w
            tiles.append(w.astype(BF16))
        spread = jnp.concatenate(
            [jnp.concatenate([w * pick for w in tiles], axis=1) for pick in picks], axis=0
        )
        values = vc[pl.ds(pl.multiple_of(c * width, width), width), :]
        return den, num + jnp.dot(spread, values, preferred_element_type=F32)

    den, num = lax.fori_loop(
        0, chunks, weigh,
        (jnp.zeros((rows, LANES), F32), jnp.zeros((n * steps, LANES), F32)),
    )
    den = lane_class_reduce(den, jnp.add, group)

    def terms(v, count):
        out = []
        for _ in range(count):
            head = v.astype(BF16).astype(F32)
            out.append(head)
            v = v - head
        return out

    side = jnp.zeros((rows, LANES), F32)
    for k, term in enumerate(terms(top, 3) + terms(den, 3)):
        side = jnp.where(lane_r // group == k, term, side)
    side = side.astype(BF16)
    num = num.astype(BF16)
    for h in range(n):
        j = h % group
        part_out[h, 0:2, :] = num[2 * h : 2 * h + 2]
        part_out[h, 2:4, :] = side[2 * j : 2 * j + 2]
    part_in[me] = part_out[me]

    def send_part(p, carry):
        peer = (me + p) % n
        pltpu.make_async_remote_copy(
            part_out.at[peer], part_in.at[me], send_sem.at[2], recv_sem.at[2],
            device_id=to(peer), device_id_type=MESH,
        ).start()
        return carry

    lax.fori_loop(1, n, send_part, 0)

    wait_all(kv_in, group - 1, 1)
    fresh = jnp.zeros((4, LANES), F32)
    for j in range(group):
        piece = kv_in[j].astype(F32)
        fresh = fresh + (pltpu.roll(piece, wide * j, 1) if j else piece)
    new_key = rotary(fresh[0:2]).astype(F32)
    new_val = fresh[2:4]
    qf = q_own.astype(F32)
    second = lax.broadcasted_iota(jnp.int32, (steps, 1), 0) > 0
    s0 = jnp.sum(qf * new_key[0:1], -1, keepdims=True) * scale
    s1 = jnp.sum(qf * new_key[1:2], -1, keepdims=True) * scale
    s1 = jnp.where(second, s1, NEG)

    wait_all(part_in, n - 1, 2)
    parts = part_in[...].astype(F32)
    lane_p = lax.broadcasted_iota(jnp.int32, (n, 2, LANES), 2)
    ours = lane_p % group == plane
    numer = parts[:, 0:2, :]
    extra = parts[:, 2:4, :]
    tops = jnp.sum(jnp.where(ours & (lane_p < 3 * group), extra, 0.0), -1, keepdims=True)
    dens = jnp.sum(
        jnp.where(ours & (lane_p >= 3 * group) & (lane_p < 6 * group), extra, 0.0), -1, keepdims=True
    )
    final = jnp.maximum(jnp.max(tops, 0), jnp.maximum(s0, s1))
    factor = jnp.exp(tops - final[None])
    w0 = jnp.exp(s0 - final)
    w1 = jnp.where(second, jnp.exp(s1 - final), 0.0)
    bottom = jnp.sum(factor * dens, 0) + w0 + w1
    upper = (
        jnp.sum(factor * numer, 0)
        + w0.astype(BF16).astype(F32) * new_val[0:1]
        + w1.astype(BF16).astype(F32) * new_val[1:2]
    )
    head_out = (upper / bottom).astype(BF16)

    loads["wo"].wait()
    span = group * LANES
    for k in range(1, n // group + 1):
        owner_plane = (plane + k) % (n // group)
        cols = pl.ds(pl.multiple_of(owner_plane * span, span), span)
        block = jnp.dot(head_out, wo[:, cols], preferred_element_type=F32).astype(BF16)
        for j in range(group):
            proj_out[owner_plane * group + j] = block[:, LANES * j : LANES * (j + 1)]

        def send_proj(j, carry, owner_plane=owner_plane):
            peer = owner_plane * group + (seat + j) % group
            pltpu.make_async_remote_copy(
                proj_out.at[peer], proj_in.at[me], send_sem.at[3], recv_sem.at[3],
                device_id=to(peer), device_id_type=MESH,
            ).start()
            return carry

        lax.fori_loop(1 if k == n // group else 0, group, send_proj, 0)
    proj_in[me] = proj_out[me]
    wait_all(proj_in, n - 1, 3)
    out_ref[...] = jnp.sum(proj_in[...].astype(F32), 0).astype(BF16)


def on_device(
    hidden, norm_gain, w_query, w_key, w_value, w_out, cache_keys, cache_values, lengths, positions
):
    n = lax.axis_size("ctx")
    steps, _, depth = hidden.shape
    _, span, group_count, head_size = cache_keys.shape
    group = n // group_count
    total = span * group_count
    chunks = 8
    half = head_size // 2
    inverse = theta_base ** (-(np.arange(half, dtype=np.float64) * 2.0 / head_size))
    inverse = np.tile(np.concatenate([inverse, inverse]).astype(np.float32)[None], (8, 1))
    dims = (n, group, steps, chunks, 1.0 / math.sqrt(head_size))
    anywhere = pl.BlockSpec(memory_space=pl.ANY)
    rows = 2 * group
    out = pl.pallas_call(
        functools.partial(kernel, dims),
        out_shape=jax.ShapeDtypeStruct((steps, w_out.shape[1] // n), BF16),
        in_specs=[anywhere] * 11,
        out_specs=pl.BlockSpec(memory_space=pltpu.VMEM),
        scratch_shapes=[
            pltpu.SMEM((1,), jnp.int32),
            pltpu.SMEM((1,), jnp.int32),
            pltpu.VMEM((steps, depth), BF16),
            pltpu.VMEM((depth // LANES, LANES), BF16),
            pltpu.VMEM((8, LANES), F32),
            pltpu.VMEM((depth, LANES), BF16),
            pltpu.VMEM((w_key.shape[1], depth), BF16),
            pltpu.VMEM((w_value.shape[1], depth), BF16),
            pltpu.VMEM(w_out.shape, BF16),
            pltpu.VMEM((total, head_size), BF16),
            pltpu.VMEM((total, head_size), BF16),
            pltpu.VMEM((n, steps, LANES), BF16),
            pltpu.VMEM((4, LANES), BF16),
            pltpu.VMEM((group, 4, LANES), BF16),
            pltpu.VMEM((chunks, rows, total // chunks), F32),
            pltpu.VMEM((n, 4, LANES), BF16),
            pltpu.VMEM((n, 4, LANES), BF16),
            pltpu.VMEM((n, steps, LANES), BF16),
            pltpu.VMEM((n, steps, LANES), BF16),
            pltpu.SemaphoreType.DMA((11,)),
            pltpu.SemaphoreType.DMA((4,)),
            pltpu.SemaphoreType.DMA((4,)),
        ],
        compiler_params=pltpu.CompilerParams(
            collective_id=0, has_side_effects=True, vmem_limit_bytes=48 * 1024 * 1024
        ),
        cost_estimate=pl.CostEstimate(flops=2**30, bytes_accessed=13 * 2**20, transcendentals=2**18),
        name="decode",
    )(
        positions,
        lengths,
        hidden.reshape(steps, depth),
        norm_gain.reshape(depth // LANES, LANES),
        jnp.asarray(inverse),
        w_query,
        w_key.T,
        w_value.T,
        w_out,
        cache_keys.reshape(total, head_size),
        cache_values.reshape(total, head_size),
    )
    return out[:, :, None]


def solution(mesh):
    in_specs = (
        P(None, "rows", None),
        P(),
        P(None, "ctx"),
        P(None, "ctx"),
        P(None, "ctx"),
        P("ctx", None),
        P("rows", "ctx", None, None),
        P("rows", "ctx", None, None),
        P("rows"),
        P("rows"),
    )
    out_specs = P(None, "ctx", "rows")
    return jax.shard_map(
        on_device, mesh=mesh, in_specs=in_specs, out_specs=out_specs, check_vma=False
    )
```

time: 267 us -> 43.7 us (0.16)
  blocking collectives: 161 us -> 0 us
  Pallas kernels: 0 us -> 34.3 us
  matrix products: 33.6 us -> 0 us
  starting transfers between devices: 23.6 us -> 0 us
  waiting for transfers between devices: 18.3 us -> 0 us
  other arithmetic: 11.3 us -> 0 us
  between operations: 7.52 us -> 1.32 us
    all_gather x4 -> x0, blocking collectives: 161 us -> none  [the longest x2 82 us: on_device(): lax.all_gather(query_local, 'ctx', axis=1, tiled=True)]
    pallas_call x0 -> x1, Pallas kernels: none -> 34.3 us  [on_device(): pl.pallas_call(functools.partial(kernel, dims), out_shape=jax.ShapeDtypeS...]
    dot_general x25 -> x0, matrix products: 33.6 us -> none  [the longest x8 13.5 us: one_block(): jnp.einsum('rkgd,rtkd->rkgt', grouped, key_block, preferred_element_type=...]
    all_to_all x4 -> x0, starting transfers between devices: 23.6 us -> none  [the longest x2 12.1 us: in_one_piece_2(): lax.all_to_all(both, axis, split_axis=split_dim, concat_axis=concat_dim,...]
    all_to_all x4 -> x0, waiting for transfers between devices: 18.3 us -> none  [the longest x2 12.6 us: sum_at_owner(): lax.all_to_all(tiles, axis, split_axis=0, concat_axis=0, tiled=True)]
    reduce_sum x16 -> x0, other arithmetic: 6.38 us -> none  [the longest x2 2.06 us: on_device(): own_den = jnp.sum(got_den * factors, 1)]
    unnamed x12 -> x15, local copies, waits for them, and re-layouts: 7.67 us -> 7.75 us
  transfers between devices with their start and end apart: 4 -> 0, of which waited for: 3 -> 0; matrix products, arithmetic and copies ran while one was open for 10% -> 0% of each run, Pallas kernels for 0% -> 0%
where the time goes in v1:
time: 43.7 us; the launch traced here: 43.3 us
  Pallas kernels  34.3 us (78%)
  local copies, waits for them, and re-layouts  7.75 us (18%)
  between operations  1.32 us (3%)
    pallas_call x1, Pallas kernels, on_device(): pl.pallas_call(functools.partial(kernel, dims), out_shape=jax.ShapeDtypeS...  34.3 us
    unnamed x15, local copies, waits for them, and re-layouts  7.75 us

profile of v1, /device:TPU:1, one launch (start us, length us, event | category | flops | bytes accessed | tf_op | source)
XLA Modules:
  0.0 43.3 jit_solution(5360273566728275817)
XLA Ops:
  1.3 0.0 copy-start
  1.3 1.6 %copy-done = bf16[8192,128]{1,0:T(8,128)(2,1)S(1)} copy-done((bf16[8192,128]{1,0:T(8,128)(2,1)S(1)}, bf16[8192,128]{1,0:T(8,128)(2,1)}, u32[]{:S(2)}) %copy-start) | copy-done | bytes 2097176
  2.9 0.0 copy-start.1
  2.9 1.6 %copy-done.1 = bf16[128,8192]{1,0:T(8,128)(2,1)S(1)} copy-done((bf16[128,8192]{1,0:T(8,128)(2,1)S(1)}, bf16[128,8192]{1,0:T(8,128)(2,1)}, u32[]{:S(2)}) %copy-start.1) | copy-done | bytes 2097176
  4.5 0.0 copy-start.2
  4.5 0.9 %copy-done.2 = bf16[8192,16]{0,1:T(8,128)(2,1)S(1)} copy-done((bf16[8192,16]{0,1:T(8,128)(2,1)S(1)}, bf16[8192,16]{0,1:T(8,128)(2,1)}, u32[]{:S(2)}) %copy-start.2) | copy-done | bytes 262168
  5.4 0.0 copy-start.3
  5.4 0.9 %copy-done.3 = bf16[8192,16]{0,1:T(8,128)(2,1)S(1)} copy-done((bf16[8192,16]{0,1:T(8,128)(2,1)S(1)}, bf16[8192,16]{0,1:T(8,128)(2,1)}, u32[]{:S(2)}) %copy-start.3) | copy-done | bytes 262168
  6.4 0.0 copy-start.4
  6.4 0.8 %copy-done.4 = bf16[2,1,8192]{2,0,1:T(2,128)(2,1)S(1)} copy-done((bf16[2,1,8192]{2,0,1:T(2,128)(2,1)S(1)}, bf16[2,1,8192]{2,0,1:T(2,128)(2,1)}, u32[]{:S(2)}) %copy-start.4) | copy-done | bytes 32792
  7.1 0.0 copy-start.5
  7.1 0.7 %copy-done.5 = bf16[8192]{0:T(1024)(128)(2,1)S(1)} copy-done((bf16[8192]{0:T(1024)(128)(2,1)S(1)}, bf16[8192]{0:T(1024)(128)(2,1)}, u32[]{:S(2)}) %copy-start.5) | copy-done | bytes 16408
  7.9 0.0 copy-start.6
  7.9 0.7 %copy-done.6 = f32[8,128]{1,0:T(8,128)S(1)} copy-done((f32[8,128]{1,0:T(8,128)S(1)}, f32[8,128]{1,0:T(8,128)}, u32[]{:S(2)}) %copy-start.6) | copy-done | bytes 4120
  8.5 34.3 %decode.1 = bf16[2,128]{1,0:T(2,128)(2,1)S(1)} custom-call(s32[1]{0:T(128)S(6)} %copy.14.pos_hbm, s32[1]{0:T(128)S(6)} %copy.13.len_hbm, bf16[2,8192]{1,0:T(2,128)(2,1)S(1)} %bitcast.9, bf16[64,128]{1,0:T(8,128)(2,1)S(1)} %bitcast.10, f32[8,128]{1,0:T(8,128)S(1)} %copy-done.6, bf16[8192,128]{1,0:T(8,128)(2,1)S(1)} %copy-done, bf16[16,8192]{1,0:T(8,128)(2,1)S(1)} %bitcast.7, ...), custom_call_target="tpu_custom_call" | custom-call | flops 1073741824 | bytes 13631488 | tf_op jit(solution)/shard_map/decode/pallas_call | solution.py:281
  42.8 0.5 %copy.15 = bf16[2,128,1]{1,0,2:T(2,128)(2,1)} copy(bf16[2,128,1]{1,0,2:T(2,128)(2,1)S(1)} %bitcast.11) | data formatting | bytes 1024
Async XLA Ops:
  1.3 1.6 %copy-start = (bf16[8192,128]{1,0:T(8,128)(2,1)S(1)}, bf16[8192,128]{1,0:T(8,128)(2,1)}, u32[]{:S(2)}) copy-start(bf16[8192,128]{1,0:T(8,128)(2,1)} %wq_hbm.1) | copy-start | bytes 6291460
  2.9 1.6 %copy-start.1 = (bf16[128,8192]{1,0:T(8,128)(2,1)S(1)}, bf16[128,8192]{1,0:T(8,128)(2,1)}, u32[]{:S(2)}) copy-start(bf16[128,8192]{1,0:T(8,128)(2,1)} %wo_hbm.1) | copy-start | bytes 6291460
  4.5 0.9 %copy-start.2 = (bf16[8192,16]{0,1:T(8,128)(2,1)S(1)}, bf16[8192,16]{0,1:T(8,128)(2,1)}, u32[]{:S(2)}) copy-start(bf16[8192,16]{0,1:T(8,128)(2,1)} %param.14) | copy-start | bytes 786436
  5.4 0.9 %copy-start.3 = (bf16[8192,16]{0,1:T(8,128)(2,1)S(1)}, bf16[8192,16]{0,1:T(8,128)(2,1)}, u32[]{:S(2)}) copy-start(bf16[8192,16]{0,1:T(8,128)(2,1)} %param.15) | copy-start | bytes 786436
  6.4 0.8 %copy-start.4 = (bf16[2,1,8192]{2,0,1:T(2,128)(2,1)S(1)}, bf16[2,1,8192]{2,0,1:T(2,128)(2,1)}, u32[]{:S(2)}) copy-start(bf16[2,1,8192]{2,0,1:T(2,128)(2,1)} %param.11) | copy-start | bytes 98308
  7.1 0.7 %copy-start.5 = (bf16[8192]{0:T(1024)(128)(2,1)S(1)}, bf16[8192]{0:T(1024)(128)(2,1)}, u32[]{:S(2)}) copy-start(bf16[8192]{0:T(1024)(128)(2,1)} %param.12) | copy-start | bytes 49156
  7.9 0.7 %copy-start.6 = (f32[8,128]{1,0:T(8,128)S(1)}, f32[8,128]{1,0:T(8,128)}, u32[]{:S(2)}) copy-start(f32[8,128]{1,0:T(8,128)} %constant.2.clone.inv_hbm) | copy-start | bytes 12292

commit v2 on v1

--- a/solution.py
+++ b/solution.py
@@ -41,28 +41,44 @@
     n, group, steps, chunks, scale = dims
     me = lax.axis_index("ctx")
     plane = me // group
-    seat = me % group
+    seat = me - plane * group
+    planes = n // group
+    half = n // 2
+
+    def each_peer(start, act):
+        for lower in start:
+            def one(i, carry, lower=lower):
+                peer = lax.rem(me + i, half) + lower
+
+                @pl.when(peer != me)
+                def _():
+                    act(peer)
+
+                return carry
+
+            lax.fori_loop(0, half, one, 0)
     rows = 2 * group
     total = kc.shape[0]
     width = total // chunks
 
     loads = {}
-    pairs = (
-        (hid_hbm, hid), (gain_hbm, gain), (pos_hbm, pos_s), (len_hbm, len_s), (inv_hbm, inv),
-        (wq_hbm, wq), (wk_hbm, wk), (wv_hbm, wv), (kc_hbm, kc), (vc_hbm, vc), (wo_hbm, wo),
-    )
-    names = ("hid", "gain", "pos", "len", "inv", "wq", "wk", "wv", "kc", "vc", "wo")
-    for i, (name, (src, dst)) in enumerate(zip(names, pairs)):
-        loads[name] = pltpu.make_async_copy(src, dst, load_sem.at[i])
-        loads[name].start()
-
+
+    def load(**pairs):
+        for name, (src, dst) in pairs.items():
+            loads[name] = pltpu.make_async_copy(src, dst, load_sem.at[len(loads)])
+            loads[name].start()
+
+    load(hid=(hid_hbm, hid), gain=(gain_hbm, gain), wq=(wq_hbm, wq), wk=(wk_hbm, wk), wv=(wv_hbm, wv))
     barrier = pltpu.get_barrier_semaphore()
 
     def greet(p, carry):
-        pl.semaphore_signal(barrier, inc=1, device_id=to((me + p) % n), device_id_type=MESH)
+        pl.semaphore_signal(barrier, inc=1, device_id=to(lax.rem(me + p, n)), device_id_type=MESH)
         return carry
 
     lax.fori_loop(1, n, greet, 0)
+
+    load(pos=(pos_hbm, pos_s), inv=(inv_hbm, inv), len=(len_hbm, len_s))
+    load(kc=(kc_hbm, kc), vc=(vc_hbm, vc), wo=(wo_hbm, wo))
 
     loads["hid"].wait()
     loads["gain"].wait()
@@ -104,7 +120,7 @@
     def send_q(p, carry):
         pltpu.make_async_remote_copy(
             q_in.at[me], q_in.at[me], send_sem.at[0], recv_sem.at[0],
-            device_id=to((me + p) % n), device_id_type=MESH,
+            device_id=to(lax.rem(me + p, n)), device_id_type=MESH,
         ).start()
         return carry
 
@@ -113,7 +129,7 @@
     def send_kv(p, carry):
         pltpu.make_async_remote_copy(
             kv_out, kv_in.at[seat], send_sem.at[1], recv_sem.at[1],
-            device_id=to(plane * group + (seat + p) % group), device_id_type=MESH,
+            device_id=to(plane * group + lax.rem(seat + p, group)), device_id_type=MESH,
         ).start()
         return carry
 
@@ -123,7 +139,7 @@
         views = buf.at[pl.ds(0, count)]
         both = pltpu.make_async_remote_copy(
             views, views, send_sem.at[k], recv_sem.at[k],
-            device_id=to((me + 1) % n), device_id_type=MESH,
+            device_id=to(lax.rem(me + 1, n)), device_id_type=MESH,
         )
         both.wait_recv()
         both.wait_send()
@@ -149,7 +165,7 @@
             top = jnp.maximum(top, mine[:, LANES * t : LANES * (t + 1)])
         return top
 
-    top = lax.fori_loop(0, chunks, score, jnp.full((rows, LANES), NEG, F32))
+    top = lax.fori_loop(0, chunks, score, jnp.full((rows, LANES), NEG, F32), unroll=True)
     top = lane_class_reduce(top, jnp.maximum, group)
 
     loads["vc"].wait()
@@ -172,7 +188,7 @@
 
     den, num = lax.fori_loop(
         0, chunks, weigh,
-        (jnp.zeros((rows, LANES), F32), jnp.zeros((n * steps, LANES), F32)),
+        (jnp.zeros((rows, LANES), F32), jnp.zeros((n * steps, LANES), F32)), unroll=True
     )
     den = lane_class_reduce(den, jnp.add, group)
 
@@ -196,7 +212,7 @@
     part_in[me] = part_out[me]
 
     def send_part(p, carry):
-        peer = (me + p) % n
+        peer = lax.rem(me + p, n)
         pltpu.make_async_remote_copy(
             part_out.at[peer], part_in.at[me], send_sem.at[2], recv_sem.at[2],
             device_id=to(peer), device_id_type=MESH,
@@ -242,22 +258,27 @@
 
     loads["wo"].wait()
     span = group * LANES
-    for k in range(1, n // group + 1):
-        owner_plane = (plane + k) % (n // group)
-        cols = pl.ds(pl.multiple_of(owner_plane * span, span), span)
-        block = jnp.dot(head_out, wo[:, cols], preferred_element_type=F32).astype(BF16)
-        for j in range(group):
-            proj_out[owner_plane * group + j] = block[:, LANES * j : LANES * (j + 1)]
-
-        def send_proj(j, carry, owner_plane=owner_plane):
-            peer = owner_plane * group + (seat + j) % group
-            pltpu.make_async_remote_copy(
-                proj_out.at[peer], proj_in.at[me], send_sem.at[3], recv_sem.at[3],
-                device_id=to(peer), device_id_type=MESH,
-            ).start()
-            return carry
-
-        lax.fori_loop(1 if k == n // group else 0, group, send_proj, 0)
+    order = list(range(planes))
+    for at in range(0, planes, 1):
+        for target in order[at : at + 1]:
+            cols = pl.ds(target * span, span)
+            block = jnp.dot(head_out, wo[:, cols], preferred_element_type=F32).astype(BF16)
+            for j in range(group):
+                proj_out[target * group + j] = block[:, LANES * j : LANES * (j + 1)]
+        for target in order[at : at + 1]:
+            def send_proj(j, carry, target=target):
+                peer = target * group + lax.rem(seat + j, group)
+
+                @pl.when(peer != me)
+                def _():
+                    pltpu.make_async_remote_copy(
+                        proj_out.at[peer], proj_in.at[me], send_sem.at[3], recv_sem.at[3],
+                        device_id=to(peer), device_id_type=MESH,
+                    ).start()
+
+                return carry
+
+            lax.fori_loop(0, group, send_proj, 0)
     proj_in[me] = proj_out[me]
     wait_all(proj_in, n - 1, 3)
     out_ref[...] = jnp.sum(proj_in[...].astype(F32), 0).astype(BF16)
@@ -278,6 +299,7 @@
     dims = (n, group, steps, chunks, 1.0 / math.sqrt(head_size))
     anywhere = pl.BlockSpec(memory_space=pl.ANY)
     rows = 2 * group
+    in_hbm = lambda a: pltpu.with_memory_space_constraint(a, pltpu.HBM)
     out = pl.pallas_call(
         functools.partial(kernel, dims),
         out_shape=jax.ShapeDtypeStruct((steps, w_out.shape[1] // n), BF16),
@@ -315,15 +337,17 @@
     )(
         positions,
         lengths,
-        hidden.reshape(steps, depth),
-        norm_gain.reshape(depth // LANES, LANES),
-        jnp.asarray(inverse),
-        w_query,
-        w_key.T,
-        w_value.T,
-        w_out,
-        cache_keys.reshape(total, head_size),
-        cache_values.reshape(total, head_size),
+        *map(in_hbm, (
+            hidden.reshape(steps, depth),
+            norm_gain.reshape(depth // LANES, LANES),
+            jnp.asarray(inverse),
+            w_query,
+            w_key.T,
+            w_value.T,
+            w_out,
+            cache_keys.reshape(total, head_size),
+            cache_values.reshape(total, head_size),
+        )),
     )
     return out[:, :, None]
 

time: 43.7 us -> 32.8 us (0.75)
  local copies, waits for them, and re-layouts: 7.75 us -> 0.51 us
  Pallas kernels: 34.3 us -> 30.9 us
    unnamed x15 -> x1, local copies, waits for them, and re-layouts: 7.75 us -> 0.51 us
    pallas_call x1, Pallas kernels: 34.3 us -> 30.9 us  [on_device(): pl.pallas_call(functools.partial(kernel, dims), out_shape=jax.ShapeDtypeS...]
where the time goes in v2:
time: 32.8 us; the launch traced here: 32.7 us
  Pallas kernels  30.9 us (94%)
  between operations  1.3 us (4%)
  local copies, waits for them, and re-layouts  0.51 us (2%)
    pallas_call x1, Pallas kernels, on_device(): pl.pallas_call(functools.partial(kernel, dims), out_shape=jax.ShapeDtypeS...  30.9 us

profile of v2, /device:TPU:1, one launch (start us, length us, event | category | flops | bytes accessed | tf_op | source)
XLA Modules:
  0.0 32.7 jit_solution(8226317582197380383)
XLA Ops:
  1.3 30.9 %decode.1 = bf16[2,128]{1,0:T(2,128)(2,1)S(1)} custom-call(s32[1]{0:T(128)S(6)} %copy.14.pos_hbm, s32[1]{0:T(128)S(6)} %copy.13.len_hbm, bf16[2,8192]{1,0:T(2,128)(2,1)} %bitcast.12, bf16[64,128]{1,0:T(8,128)(2,1)} %bitcast.13, f32[8,128]{1,0:T(8,128)} %constant.2.clone.inv_hbm, bf16[8192,128]{1,0:T(8,128)(2,1)} %wq_hbm.1, bf16[16,8192]{1,0:T(8,128)(2,1)} %bitcast.10, ...), custom_call_target="tpu_custom_call" | custom-call | flops 1073741824 | bytes 13631488 | tf_op jit(solution)/shard_map/decode/pallas_call | solution.py:303
  32.2 0.5 %copy.15 = bf16[2,128,1]{1,0,2:T(2,128)(2,1)} copy(bf16[2,128,1]{1,0,2:T(2,128)(2,1)S(1)} %bitcast.7) | data formatting | bytes 1024

commit v3 on v2

--- a/solution.py
+++ b/solution.py
@@ -43,20 +43,6 @@
     plane = me // group
     seat = me - plane * group
     planes = n // group
-    half = n // 2
-
-    def each_peer(start, act):
-        for lower in start:
-            def one(i, carry, lower=lower):
-                peer = lax.rem(me + i, half) + lower
-
-                @pl.when(peer != me)
-                def _():
-                    act(peer)
-
-                return carry
-
-            lax.fori_loop(0, half, one, 0)
     rows = 2 * group
     total = kc.shape[0]
     width = total // chunks
@@ -75,7 +61,7 @@
         pl.semaphore_signal(barrier, inc=1, device_id=to(lax.rem(me + p, n)), device_id_type=MESH)
         return carry
 
-    lax.fori_loop(1, n, greet, 0)
+    lax.fori_loop(1, n, greet, 0, unroll=9)
 
     load(pos=(pos_hbm, pos_s), inv=(inv_hbm, inv), len=(len_hbm, len_s))
     load(kc=(kc_hbm, kc), vc=(vc_hbm, vc), wo=(wo_hbm, wo))
@@ -124,7 +110,7 @@
         ).start()
         return carry
 
-    lax.fori_loop(1, n, send_q, 0)
+    lax.fori_loop(1, n, send_q, 0, unroll=9)
 
     def send_kv(p, carry):
         pltpu.make_async_remote_copy(
@@ -133,7 +119,7 @@
         ).start()
         return carry
 
-    lax.fori_loop(1, group, send_kv, 0)
+    lax.fori_loop(1, group, send_kv, 0, unroll=True)
 
     def wait_all(buf, count, k):
         views = buf.at[pl.ds(0, count)]
@@ -219,7 +205,7 @@
         ).start()
         return carry
 
-    lax.fori_loop(1, n, send_part, 0)
+    lax.fori_loop(1, n, send_part, 0, unroll=9)
 
     wait_all(kv_in, group - 1, 1)
     fresh = jnp.zeros((4, LANES), F32)
@@ -259,6 +245,13 @@
     loads["wo"].wait()
     span = group * LANES
     order = list(range(planes))
+
+    def send_proj(peer):
+        pltpu.make_async_remote_copy(
+            proj_out.at[peer], proj_in.at[me], send_sem.at[3], recv_sem.at[3],
+            device_id=to(peer), device_id_type=MESH,
+        ).start()
+
     for at in range(0, planes, 1):
         for target in order[at : at + 1]:
             cols = pl.ds(target * span, span)
@@ -266,19 +259,13 @@
             for j in range(group):
                 proj_out[target * group + j] = block[:, LANES * j : LANES * (j + 1)]
         for target in order[at : at + 1]:
-            def send_proj(j, carry, target=target):
-                peer = target * group + lax.rem(seat + j, group)
-
-                @pl.when(peer != me)
-                def _():
-                    pltpu.make_async_remote_copy(
-                        proj_out.at[peer], proj_in.at[me], send_sem.at[3], recv_sem.at[3],
-                        device_id=to(peer), device_id_type=MESH,
-                    ).start()
-
-                return carry
-
-            lax.fori_loop(0, group, send_proj, 0)
+            for j in range(1, group):
+                send_proj(target * group + lax.rem(seat + j, group))
+    for target in order:
+        @pl.when(target != plane)
+        def _(target=target):
+            send_proj(target * group + seat)
+
     proj_in[me] = proj_out[me]
     wait_all(proj_in, n - 1, 3)
     out_ref[...] = jnp.sum(proj_in[...].astype(F32), 0).astype(BF16)

time: 32.8 us -> 32.5 us (level)
  no operation moved by 1% of the time
where the time goes in v3:
time: 32.5 us; the launch traced here: 32.4 us
  Pallas kernels  30.6 us (94%)
  between operations  1.3 us (4%)
  local copies, waits for them, and re-layouts  0.51 us (2%)
    pallas_call x1, Pallas kernels, on_device(): pl.pallas_call(functools.partial(kernel, dims), out_shape=jax.ShapeDtypeS...  30.6 us

profile of v3, /device:TPU:1, one launch (start us, length us, event | category | flops | bytes accessed | tf_op | source)
XLA Modules:
  0.0 32.4 jit_solution(3561657003827763377)
XLA Ops:
  1.3 30.6 %decode.1 = bf16[2,128]{1,0:T(2,128)(2,1)S(1)} custom-call(s32[1]{0:T(128)S(6)} %copy.14.pos_hbm, s32[1]{0:T(128)S(6)} %copy.13.len_hbm, bf16[2,8192]{1,0:T(2,128)(2,1)} %bitcast.12, bf16[64,128]{1,0:T(8,128)(2,1)} %bitcast.13, f32[8,128]{1,0:T(8,128)} %constant.2.clone.inv_hbm, bf16[8192,128]{1,0:T(8,128)(2,1)} %wq_hbm.1, bf16[16,8192]{1,0:T(8,128)(2,1)} %bitcast.10, ...), custom_call_target="tpu_custom_call" | custom-call | flops 1073741824 | bytes 13631488 | tf_op jit(solution)/shard_map/decode/pallas_call | solution.py:290
  31.9 0.5 %copy.15 = bf16[2,128,1]{1,0,2:T(2,128)(2,1)} copy(bf16[2,128,1]{1,0,2:T(2,128)(2,1)S(1)} %bitcast.7) | data formatting | bytes 1024

commit v4 on v3

--- a/solution.py
+++ b/solution.py
@@ -36,13 +36,16 @@
     out_ref,
     pos_s, len_s, hid, gain, inv, wq, wk, wv, wo, kc, vc,
     q_in, kv_out, kv_in, scores, part_out, part_in, proj_out, proj_in,
-    load_sem, send_sem, recv_sem,
+    load_sem, send_sem, recv_sem, q_sem, ready,
 ):
     n, group, steps, chunks, scale = dims
     me = lax.axis_index("ctx")
     plane = me // group
     seat = me - plane * group
     planes = n // group
+    half = n // 2
+    upper = plane >= planes // 2
+    lower = plane < planes // 2
     rows = 2 * group
     total = kc.shape[0]
     width = total // chunks
@@ -57,11 +60,31 @@
     load(hid=(hid_hbm, hid), gain=(gain_hbm, gain), wq=(wq_hbm, wq), wk=(wk_hbm, wk), wv=(wv_hbm, wv))
     barrier = pltpu.get_barrier_semaphore()
 
-    def greet(p, carry):
-        pl.semaphore_signal(barrier, inc=1, device_id=to(lax.rem(me + p, n)), device_id_type=MESH)
-        return carry
-
-    lax.fori_loop(1, n, greet, 0, unroll=9)
+    def others(start, act):
+        def one(p, carry):
+            act(lax.rem(me + p, half) + start)
+            return carry
+
+        lax.fori_loop(1, half, one, 0, unroll=half - 1)
+
+    def across(start, act):
+        def one(p, carry):
+            act(lax.rem(me + p, half) + start)
+            return carry
+
+        lax.fori_loop(0, half, one, 0, unroll=half)
+
+    def greet(peer):
+        pl.semaphore_signal(barrier, inc=1, device_id=to(peer), device_id_type=MESH)
+
+    @pl.when(lower)
+    def _():
+        others(0, greet)
+        across(half, greet)
+
+    @pl.when(upper)
+    def _():
+        others(half, greet)
 
     load(pos=(pos_hbm, pos_s), inv=(inv_hbm, inv), len=(len_hbm, len_s))
     load(kc=(kc_hbm, kc), vc=(vc_hbm, vc), wo=(wo_hbm, wo))
@@ -101,16 +124,68 @@
     q_in[me] = q_own
     kv_in[seat] = kv_out[...]
 
-    pl.semaphore_wait(barrier, n - 1)
-
-    def send_q(p, carry):
-        pltpu.make_async_remote_copy(
-            q_in.at[me], q_in.at[me], send_sem.at[0], recv_sem.at[0],
-            device_id=to(lax.rem(me + p, n)), device_id_type=MESH,
+    def send_q(k):
+        def one(peer):
+            pltpu.make_async_remote_copy(
+                q_in.at[me], q_in.at[me], send_sem.at[0], q_sem.at[k],
+                device_id=to(peer), device_id_type=MESH,
+            ).start()
+
+        return one
+
+    def queries_come(k, count):
+        come = q_in.at[pl.ds(0, count)]
+        pltpu.make_async_remote_copy(
+            come, come, send_sem.at[0], q_sem.at[k],
+            device_id=to(lax.rem(me + 1, n)), device_id_type=MESH,
+        ).wait_recv()
+
+    def queries_left(count):
+        come = q_in.at[pl.ds(0, count)]
+        pltpu.make_async_remote_copy(
+            come, come, send_sem.at[0], q_sem.at[0],
+            device_id=to(lax.rem(me + 1, n)), device_id_type=MESH,
+        ).wait_send()
+
+    quarter = planes // 4
+    far = planes - quarter
+    first_relay, last_relay = planes // 2 - 1, 0
+
+    def relay(peer, slot):
+        pl.semaphore_wait(ready.at[slot], 1)
+        pltpu.make_async_remote_copy(
+            q_in.at[pl.ds(0, half)], q_in.at[pl.ds(0, half)], send_sem.at[4 + slot], q_sem.at[0],
+            device_id=to(peer), device_id_type=MESH,
         ).start()
-        return carry
-
-    lax.fori_loop(1, n, send_q, 0, unroll=9)
+
+    @pl.when(lower)
+    def _():
+        pl.semaphore_wait(barrier, half - 1)
+        others(0, send_q(0))
+        queries_come(0, half - 1)
+
+    for where, start in ((first_relay, planes // 2), (last_relay, far)):
+        @pl.when(plane == where)
+        def _(start=start):
+            for slot in range(quarter):
+                relay((start + slot) * group + seat, slot)
+
+    @pl.when(upper)
+    def _():
+        pl.semaphore_wait(barrier, n - 1)
+
+    for start, where in ((planes // 2, first_relay), (far, last_relay)):
+        for slot in range(quarter):
+            @pl.when(plane == start + slot)
+            def _(slot=slot, where=where):
+                pl.semaphore_signal(
+                    ready.at[slot], inc=1, device_id=to(where * group + seat), device_id_type=MESH
+                )
+
+    @pl.when(upper)
+    def _():
+        others(half, send_q(1))
+        across(0, send_q(1))
 
     def send_kv(p, carry):
         pltpu.make_async_remote_copy(
@@ -132,7 +207,28 @@
 
     loads["kc"].wait()
     loads["len"].wait()
-    wait_all(q_in, n - 1, 0)
+
+    @pl.when(lower)
+    def _():
+        queries_come(1, half)
+        queries_left(half - 1)
+
+    for where in (first_relay, last_relay):
+        @pl.when(plane == where)
+        def _():
+            for slot in range(quarter):
+                block = q_in.at[pl.ds(0, half)]
+                pltpu.make_async_remote_copy(
+                    block, block, send_sem.at[4 + slot], q_sem.at[0],
+                    device_id=to(lax.rem(me + 1, n)), device_id_type=MESH,
+                ).wait_send()
+
+    @pl.when(upper)
+    def _():
+        queries_come(1, half - 1)
+        queries_come(0, half)
+        queries_left(n - 1)
+
 
     live = jnp.clip(len_s[0] - me * (total // group), 0, total // group) * group
     lane_w = lax.broadcasted_iota(jnp.int32, (rows, width), 1)
@@ -279,7 +375,7 @@
     _, span, group_count, head_size = cache_keys.shape
     group = n // group_count
     total = span * group_count
-    chunks = 8
+    chunks = 16
     half = head_size // 2
     inverse = theta_base ** (-(np.arange(half, dtype=np.float64) * 2.0 / head_size))
     inverse = np.tile(np.concatenate([inverse, inverse]).astype(np.float32)[None], (8, 1))
@@ -313,8 +409,10 @@
             pltpu.VMEM((n, steps, LANES), BF16),
             pltpu.VMEM((n, steps, LANES), BF16),
             pltpu.SemaphoreType.DMA((11,)),
+            pltpu.SemaphoreType.DMA((4 + group_count // 4,)),
             pltpu.SemaphoreType.DMA((4,)),
-            pltpu.SemaphoreType.DMA((4,)),
+            pltpu.SemaphoreType.DMA((2,)),
+            pltpu.SemaphoreType.REGULAR((group_count // 4,)),
         ],
         compiler_params=pltpu.CompilerParams(
             collective_id=0, has_side_effects=True, vmem_limit_bytes=48 * 1024 * 1024

time: 32.5 us -> 32.4 us (level)
  no operation moved by 1% of the time
where the time goes in v4:
time: 32.4 us; the launch traced here: 32.3 us
  Pallas kernels  30.5 us (94%)
  between operations  1.3 us (4%)
  local copies, waits for them, and re-layouts  0.51 us (2%)
    pallas_call x1, Pallas kernels, on_device(): pl.pallas_call(functools.partial(kernel, dims), out_shape=jax.ShapeDtypeS...  30.5 us

profile of v4, /device:TPU:1, one launch (start us, length us, event | category | flops | bytes accessed | tf_op | source)
XLA Modules:
  0.0 32.3 jit_solution(10052161913818893085)
XLA Ops:
  1.3 30.5 %decode.1 = bf16[2,128]{1,0:T(2,128)(2,1)S(1)} custom-call(s32[1]{0:T(128)S(6)} %copy.14.pos_hbm, s32[1]{0:T(128)S(6)} %copy.13.len_hbm, bf16[2,8192]{1,0:T(2,128)(2,1)} %bitcast.12, bf16[64,128]{1,0:T(8,128)(2,1)} %bitcast.13, f32[8,128]{1,0:T(8,128)} %constant.2.clone.inv_hbm, bf16[8192,128]{1,0:T(8,128)(2,1)} %wq_hbm.1, bf16[16,8192]{1,0:T(8,128)(2,1)} %bitcast.10, ...), custom_call_target="tpu_custom_call" | custom-call | flops 1073741824 | bytes 13631488 | tf_op jit(solution)/shard_map/decode/pallas_call | solution.py:386
  31.8 0.5 %copy.15 = bf16[2,128,1]{1,0,2:T(2,128)(2,1)} copy(bf16[2,128,1]{1,0,2:T(2,128)(2,1)S(1)} %bitcast.7) | data formatting | bytes 1024
